TPU v7x, 32 devices: a whole 2x2x4 slice. The times are simulated.
32 devices in a mesh: dp: 8 (over y, x, core), ctx: 4 (over z).
Axes of the slice: x: 2, y: 2, z: 4, core: 2. Of those that a mesh axis runs over, the one named last changes fastest.
Arguments:
- inputs: bfloat16 [8, 1024, 2048], P('dp', 'ctx'), may hold values from -6 to 6
- lengths: int32 [8], P('dp'), may hold values from 512 to 1024, as said below
- norm_gain: bfloat16 [2048], replicated, may hold values from 0.5 to 1.5
- up_weight: bfloat16 [2048, 8192], P('dp'), may hold values from -0.125 to 0.125
- conv_weight: bfloat16 [4, 4096], replicated, may hold values from -3 to 3
- conv_bias: bfloat16 [4096], replicated, may hold values from -3 to 3
- qkv_weight: bfloat16 [3, 4, 4, 4, 256], replicated, may hold values from -3 to 3
- gate_weight: bfloat16 [8, 12288], replicated, may hold values from -0.109375 to 0.109375
- gate_bias: bfloat16 [8], replicated, may hold values from -1 to 8.5
- skip_weight: bfloat16 [4096], replicated, may hold values from 0.5 to 1.5
- outnorm_weight: bfloat16 [4096], replicated, may hold values from 0.5 to 1.5
- down_weight: bfloat16 [4096, 2048], P('dp'), may hold values from -0.09375 to 0.09375
- grad_out: bfloat16 [8, 1024, 2048], P('dp', 'ctx'), may hold values from -6 to 6
Outputs:
- outputs: bfloat16 [8, 1024, 2048], P('dp', 'ctx')
- grad_inputs: float32 [8, 1024, 2048], P('dp', 'ctx')
- grad_norm_gain: float32 [2048], replicated
- grad_up_weight: float32 [2048, 8192], P('dp')
- grad_conv_weight: float32 [4, 4096], replicated
- grad_conv_bias: float32 [4096], replicated
- grad_qkv_weight: float32 [3, 4, 4, 4, 256], replicated
- grad_gate_weight: float32 [8, 12288], replicated
- grad_gate_bias: float32 [8], replicated
- grad_skip_weight: float32 [4096], replicated
- grad_outnorm_weight: float32 [4096], replicated
- grad_down_weight: float32 [4096, 2048], P('dp')
Inputs may be any that keep to these rules, and one draw needn't show every extreme that they name: `lengths`: each entry counts the real tokens of a sequence from its start; one sequence has exactly 1024, another exactly 512.
All inputs are finite; a program needn't handle non-finite values.
Results may differ from a plain program's by a relative error of at most 0.04.
Values may be sent and summed in bfloat16 or wider, within the bound.
No kernel may reach another device: no remote copies, remote signals or barrier semaphores. Data moves between devices by JAX's collectives and lax.ppermute only.
A program may use at most 448 MiB of HBM per device.

v0:
```python
from functools import partial
import jax
import jax.numpy as jnp
from jax import lax
from jax.sharding import PartitionSpec as P

highest = lax.Precision.HIGHEST
epsilon = 1e-05


def shifted(x, axis, by):
    length = lax.axis_size(axis)
    pairs = [(i, i + by) for i in range(length) if 0 <= i + by < length]
    return lax.ppermute(x, axis, pairs)


def low(value_in):
    rounded = lax.optimization_barrier(value_in.astype(jnp.bfloat16)).astype(jnp.float32)
    return value_in + lax.stop_gradient(rounded - value_in)


def layer_norm_low(rows_in, gain_row):
    centred = rows_in - jnp.mean(rows_in, axis=-1, keepdims=True)
    spread = jnp.mean(centred * centred, axis=-1, keepdims=True)
    return low(centred * lax.rsqrt(spread + epsilon) * gain_row)


def headwise(values_in, blocks_in):
    row_count, width_all = values_in.shape
    head_count, block_size, block_out, block_count = blocks_in.shape
    grouped = values_in.reshape(row_count, head_count, block_size, block_count)
    mixed_rows = jnp.einsum("thij,hioj->thoj", grouped, blocks_in, precision=highest)
    return mixed_rows.reshape(row_count, width_all)


def split_heads(rows_in, head_count):
    return rows_in.reshape(rows_in.shape[0], head_count, -1).transpose(1, 0, 2)


def mid_section(mixer_in, rim_rows, conv_taps, conv_shift, qkv_blocks, gate_matrix, gate_offset):
    row_count, width_all = mixer_in.shape
    kernel_size = conv_taps.shape[0]
    head_count = qkv_blocks.shape[1]
    padded_in = jnp.concatenate([rim_rows, mixer_in], axis=0)
    conv_pre = conv_shift[None, :] + conv_taps[0][None, :] * padded_in[0:row_count]
    for tap_index in range(1, kernel_size):
        conv_pre = (
            conv_pre + conv_taps[tap_index][None, :] * padded_in[tap_index : tap_index + row_count]
        )
    conv_out = jax.nn.silu(conv_pre)
    key_scale = (width_all // head_count) ** (-0.5)
    queries = low(headwise(conv_out, qkv_blocks[0]))
    key_rows = low(headwise(conv_out, qkv_blocks[1]) * key_scale)
    value_rows = low(headwise(mixer_in, qkv_blocks[2]))
    joined = jnp.concatenate([queries, key_rows, value_rows], axis=1)
    gate_pre = jnp.dot(joined, gate_matrix.T, precision=highest) + gate_offset[None, :]
    return (
        queries,
        key_rows,
        value_rows,
        gate_pre[:, :head_count],
        jax.nn.log_sigmoid(gate_pre[:, head_count:]),
        conv_out,
    )


def cell_scores(queries, key_rows, head_count):
    return jnp.einsum(
        "htk,hsk->hts",
        split_heads(queries, head_count),
        split_heads(key_rows, head_count),
        precision=highest,
    )


def cell_rest(scores, queries, value_rows, in_gate, log_forget, state_in):
    row_count, width_all = queries.shape
    head_count = state_in.shape[0]
    query_heads = split_heads(queries, head_count)
    value_heads = split_heads(value_rows, head_count)
    decay_sum = jnp.cumsum(log_forget, axis=0).T
    gate_row = in_gate.T
    causal = jnp.arange(row_count)[:, None] >= jnp.arange(row_count)[None, :]
    exponent = decay_sum[:, :, None] - decay_sum[:, None, :] + gate_row[:, None, :]
    weights = jnp.where(causal[None], jnp.exp(jnp.where(causal[None], exponent, 0.0)), 0.0)
    mix_weights = low(weights * scores)
    within = jnp.einsum("hts,hsd->htd", mix_weights, value_heads, precision=highest)
    carried = jnp.einsum("htk,hkd->htd", query_heads, low(state_in), precision=highest)
    numerator = within + jnp.exp(decay_sum)[:, :, None] * carried
    return numerator.transpose(1, 0, 2).reshape(row_count, width_all)


def summary(key_rows, value_rows, in_gate, log_forget):
    head_count = in_gate.shape[1]
    decay_sum = jnp.cumsum(log_forget, axis=0)
    span_decay = decay_sum[-1]
    weights = jnp.exp(span_decay[None, :] - decay_sum + in_gate)
    weighted = low(split_heads(key_rows, head_count) * weights.T[:, :, None])
    state_part = jnp.einsum(
        "htk,htd->hkd", weighted, split_heads(value_rows, head_count), precision=highest
    )
    return (state_part, span_decay)


def tail_section(numerator, conv_out, gate_in, outnorm_scale, skip_scale, head_count):
    row_count, width_all = numerator.shape
    grouped = numerator.reshape(row_count, head_count, -1)
    centred = grouped - jnp.mean(grouped, axis=-1, keepdims=True)
    spread = jnp.mean(centred * centred, axis=-1, keepdims=True)
    normed = (centred * lax.rsqrt(spread + epsilon)).reshape(row_count, width_all) * outnorm_scale
    return low((normed + skip_scale * conv_out) * jax.nn.silu(gate_in))


def on_device(
    inputs,
    lengths,
    norm_gain,
    up_weight,
    conv_weight,
    conv_bias,
    qkv_weight,
    gate_weight,
    gate_bias,
    skip_weight,
    outnorm_weight,
    down_weight,
    grad_out,
):
    span_len = inputs.shape[1]
    inner_width = conv_weight.shape[1]
    head_count = qkv_weight.shape[1]
    kernel_size = conv_weight.shape[0]
    ctx_count = lax.axis_size("ctx")
    ctx_index = lax.axis_index("ctx")
    positions = ctx_index * span_len + jnp.arange(span_len)
    live_rows = (positions < lengths[0]).astype(jnp.float32)[:, None]
    rows_in = inputs[0].astype(jnp.float32)
    norm_scale = norm_gain.astype(jnp.float32)
    conv_taps = conv_weight.astype(jnp.float32)
    conv_shift = conv_bias.astype(jnp.float32)
    qkv_blocks = qkv_weight.astype(jnp.float32)
    gate_matrix = gate_weight.astype(jnp.float32)
    gate_offset = gate_bias.astype(jnp.float32)
    skip_scale = skip_weight.astype(jnp.float32)
    outnorm_scale = outnorm_weight.astype(jnp.float32)
    contract_last = (((1,), (1,)), ((), ()))
    contract_first = (((0,), (0,)), ((), ()))
    normed, front_back = jax.vjp(layer_norm_low, rows_in, norm_scale)
    normed_low = normed.astype(jnp.bfloat16)
    columns = normed_low
    upward = jnp.dot(
        columns,
        lax.all_gather(up_weight, "dp", axis=0, tiled=True),
        preferred_element_type=jnp.float32,
    )
    mixer_low = upward[:, :inner_width].astype(jnp.bfloat16)
    mixer_in = mixer_low.astype(jnp.float32)
    gate_in = upward[:, inner_width:]
    rim_rows = shifted(mixer_low[span_len - kernel_size + 1 :], "ctx", 1).astype(jnp.float32)
    mid_result, mid_back = jax.vjp(
        mid_section, mixer_in, rim_rows, conv_taps, conv_shift, qkv_blocks, gate_matrix, gate_offset
    )
    queries, key_rows, value_rows, in_gate, log_forget, conv_out = mid_result
    summed, summary_back = jax.vjp(summary, key_rows, value_rows, in_gate, log_forget)
    state_part, span_decay = summed

    def relay(turn, carried):
        return shifted(jnp.exp(span_decay)[:, None, None] * carried + state_part, "ctx", 1)

    state_in = lax.fori_loop(0, ctx_count - 1, relay, jnp.zeros_like(state_part))
    scores, score_back = jax.vjp(partial(cell_scores, head_count=head_count), queries, key_rows)
    numerator, rest_back = jax.vjp(
        cell_rest, scores, queries, value_rows, in_gate, log_forget, state_in
    )
    hidden_state, tail_back = jax.vjp(
        partial(tail_section, head_count=head_count),
        numerator,
        conv_out,
        gate_in,
        outnorm_scale,
        skip_scale,
    )
    hidden_low = hidden_state.astype(jnp.bfloat16)
    columns = hidden_low
    branch = jnp.dot(
        columns,
        lax.all_gather(down_weight, "dp", axis=0, tiled=True),
        preferred_element_type=jnp.float32,
    )
    outputs = (live_rows * (rows_in + branch)).astype(jnp.bfloat16)[None]
    out_grad = grad_out[0].astype(jnp.float32) * live_rows
    branch_grad = out_grad.astype(jnp.bfloat16)
    hidden_grad = lax.dot_general(
        branch_grad,
        lax.all_gather(down_weight, "dp", axis=0, tiled=True),
        contract_last,
        preferred_element_type=jnp.float32,
    )
    numer_raw, conv_tail_grad, gate_in_grad, outnorm_grad, skip_grad = tail_back(hidden_grad)
    numer_low = numer_raw.astype(jnp.bfloat16)
    numer_grad = numer_low.astype(jnp.float32)
    scores_raw, query_part, value_grad, ingate_grad, forget_grad, state_grad = rest_back(numer_grad)
    query_extra, key_grad = score_back(scores_raw.astype(jnp.bfloat16).astype(jnp.float32))
    query_grad = query_part + query_extra

    def relay_back(turn, carried):
        return shifted(jnp.exp(span_decay)[:, None, None] * carried + state_grad, "ctx", -1)

    later_grad = lax.fori_loop(0, ctx_count - 1, relay_back, jnp.zeros_like(state_grad))
    decay_grad = jnp.exp(span_decay) * jnp.sum(later_grad * state_in, axis=(1, 2))
    later_rounded = later_grad.astype(jnp.bfloat16).astype(jnp.float32)
    key_extra, value_extra, ingate_extra, forget_extra = summary_back((later_rounded, decay_grad))
    mid_grads = mid_back(
        (
            query_grad,
            key_grad + key_extra,
            value_grad + value_extra,
            ingate_grad + ingate_extra,
            forget_grad + forget_extra,
            conv_tail_grad,
        )
    )
    (
        mixer_grad,
        rim_grad,
        conv_taps_grad,
        conv_shift_grad,
        qkv_grad,
        gate_matrix_grad,
        gate_offset_grad,
    ) = mid_grads
    rim_returned = shifted(rim_grad.astype(jnp.bfloat16), "ctx", -1).astype(rim_grad.dtype)
    mixer_grad = mixer_grad + jnp.pad(rim_returned, ((span_len - kernel_size + 1, 0), (0, 0)))
    upward_grad = jnp.concatenate([mixer_grad, gate_in_grad], axis=1).astype(jnp.bfloat16)
    normed_grad = lax.dot_general(
        upward_grad,
        lax.all_gather(up_weight, "dp", axis=0, tiled=True),
        contract_last,
        preferred_element_type=jnp.float32,
    )
    front_grad, norm_scale_grad = front_back(normed_grad)
    input_grad = (out_grad + front_grad)[None]
    columns = normed_low
    up_part = lax.psum_scatter(
        lax.dot_general(
            columns, upward_grad, contract_first, preferred_element_type=jnp.float32
        ).astype(jnp.bfloat16),
        "dp",
        scatter_dimension=0,
        tiled=True,
    )
    columns = hidden_low
    down_part = lax.psum_scatter(
        lax.dot_general(
            columns, branch_grad, contract_first, preferred_element_type=jnp.float32
        ).astype(jnp.bfloat16),
        "dp",
        scatter_dimension=0,
        tiled=True,
    )
    up_total, down_total = (
        lax.psum(up_part, "ctx").astype(jnp.float32),
        lax.psum(down_part, "ctx").astype(jnp.float32),
    )
    small_total = lax.psum(
        (
            norm_scale_grad,
            conv_taps_grad,
            conv_shift_grad,
            qkv_grad,
            gate_matrix_grad,
            gate_offset_grad,
            skip_grad,
            outnorm_grad,
        ),
        ("dp", "ctx"),
    )
    return (
        outputs,
        input_grad,
        small_total[0],
        up_total,
        small_total[1],
        small_total[2],
        small_total[3],
        small_total[4],
        small_total[5],
        small_total[6],
        small_total[7],
        down_total,
    )


def solution(mesh):
    return jax.shard_map(
        on_device,
        mesh=mesh,
        in_specs=(
            P("dp", "ctx", None),
            P("dp"),
            P(),
            P("dp", None),
            P(),
            P(),
            P(),
            P(),
            P(),
            P(),
            P(),
            P("dp", None),
            P("dp", "ctx", None),
        ),
        out_specs=(
            P("dp", "ctx", None),
            P("dp", "ctx", None),
            P(),
            P("dp", None),
            P(),
            P(),
            P(),
            P(),
            P(),
            P(),
            P(),
            P("dp", None),
        ),
        check_vma=False,
    )
```

profile of v0, /device:TPU:0, one launch (start us, length us, event | category | flops | bytes accessed | tf_op | source)
XLA Modules:
  0.0 3726.6 jit_solution(15394948117392416776)
XLA Ops:
  16.5 157.0 %all-gather.3.cloned.1.call-done = bf16[2048,8192]{1,0:T(8,128)(2,1)} async-done(((bf16[256,8192]{1,0:T(8,128)(2,1)}), bf16[2048,8192]{1,0:T(8,128)(2,1)}) %all-gather.3.cloned.1.call-update) | async-done | bytes 33554448 | tf_op jit(solution)/shard_map/all_gather | solution.py:153
  173.5 19.8 fusion.142
  214.1 51.2 %all-gather.5.cloned.1.call-done = bf16[4096,2048]{1,0:T(8,128)(2,1)} async-done(((bf16[512,2048]{1,0:T(8,128)(2,1)}), bf16[4096,2048]{1,0:T(8,128)(2,1)}) %all-gather.5.cloned.1.call-update) | async-done | bytes 16777232 | tf_op jit(solution)/shard_map/all_gather | solution.py:187
  265.3 12.3 broadcast_multiply_fusion
  344.5 10.2 fusion.100
  357.9 29.3 fusion.54
  387.1 8.0 broadcast.160.clone
  395.1 1142.1 %while.24 = (s32[]{:T(128)}, f32[4,1024,1024]{2,1,0:T(8,128)}, f32[4,1,1]{0,2,1:T(1,128)S(1)}, f32[4,1024,1024]{2,1,0:T(8,128)}, s32[]{:T(128)}) while((s32[]{:T(128)}, f32[4,1024,1024]{2,1,0:T(8,128)}, f32[4,1,1]{0,2,1:T(1,128)S(1)}, f32[4,1024,1024]{2,1,0:T(8,128)}, s32[]{:T(128)}) %tuple.133), condition=%wide.region_5.6_spmd, body=%wide.region_4.5_spmd.sunk | while | flops 8388610 | bytes 117440624 | solution.py:170
  395.1 17.3 multiply_add_fusion.10
  412.4 9.2 collective-permute-start
  421.7 354.4 %collective-permute-done = f32[4,1024,1024]{2,1,0:T(8,128)} collective-permute-done((f32[4,1024,1024]{2,1,0:T(8,128)}, f32[4,1024,1024]{2,1,0:T(8,128)}, u32[]{:S(2)}, u32[]{:S(2)}) %collective-permute-start) | collective-permute-done | bytes 16777248 | tf_op jit(solution)/shard_map/while/body/eval_jaxpr/ppermute | solution.py:14
  776.0 17.3 multiply_add_fusion.10
  793.3 10.2 collective-permute-start
  803.6 353.6 %collective-permute-done = f32[4,1024,1024]{2,1,0:T(8,128)} collective-permute-done((f32[4,1024,1024]{2,1,0:T(8,128)}, f32[4,1024,1024]{2,1,0:T(8,128)}, u32[]{:S(2)}, u32[]{:S(2)}) %collective-permute-start) | collective-permute-done | bytes 16777248 | tf_op jit(solution)/shard_map/while/body/eval_jaxpr/ppermute | solution.py:14
  1157.1 17.3 multiply_add_fusion.10
  1174.4 10.2 collective-permute-start
  1184.6 352.6 %collective-permute-done = f32[4,1024,1024]{2,1,0:T(8,128)} collective-permute-done((f32[4,1024,1024]{2,1,0:T(8,128)}, f32[4,1024,1024]{2,1,0:T(8,128)}, u32[]{:S(2)}, u32[]{:S(2)}) %collective-permute-start) | collective-permute-done | bytes 16777248 | tf_op jit(solution)/shard_map/while/body/eval_jaxpr/ppermute | solution.py:14
  1537.3 9.3 convert_element_type.160
  1547.3 22.0 fusion.1
  1569.3 12.2 fusion.143
  1591.8 21.5 fusion
  1613.3 18.2 fusion.4
  1639.4 1136.2 %while.25 = (s32[]{:T(128)}, f32[4,1024,1024]{2,1,0:T(8,128)}, f32[4,1,1]{0,2,1:T(1,128)S(1)}, f32[4,1024,1024]{2,1,0:T(8,128)}, s32[]{:T(128)}) while((s32[]{:T(128)}, f32[4,1024,1024]{2,1,0:T(8,128)}, f32[4,1,1]{0,2,1:T(1,128)S(1)}, f32[4,1024,1024]{2,1,0:T(8,128)}, s32[]{:T(128)}) %tuple.134), condition=%wide.region_11.12_spmd, body=%wide.region_10.11_spmd.sunk | while | flops 8388610 | bytes 117440624 | solution.py:209
  1639.4 17.3 multiply_add_fusion.11
  1658.0 361.4 %collective-permute-done.1 = f32[4,1024,1024]{2,1,0:T(8,128)} collective-permute-done((f32[4,1024,1024]{2,1,0:T(8,128)}, f32[4,1024,1024]{2,1,0:T(8,128)}, u32[]{:S(2)}, u32[]{:S(2)}) %collective-permute-start.1) | collective-permute-done | bytes 16777248 | tf_op jit(solution)/shard_map/while/body/eval_jaxpr/ppermute | solution.py:14
  2019.4 17.3 multiply_add_fusion.11
  2038.0 360.0 %collective-permute-done.1 = f32[4,1024,1024]{2,1,0:T(8,128)} collective-permute-done((f32[4,1024,1024]{2,1,0:T(8,128)}, f32[4,1024,1024]{2,1,0:T(8,128)}, u32[]{:S(2)}, u32[]{:S(2)}) %collective-permute-start.1) | collective-permute-done | bytes 16777248 | tf_op jit(solution)/shard_map/while/body/eval_jaxpr/ppermute | solution.py:14
  2398.0 17.3 multiply_add_fusion.11
  2416.6 359.1 %collective-permute-done.1 = f32[4,1024,1024]{2,1,0:T(8,128)} collective-permute-done((f32[4,1024,1024]{2,1,0:T(8,128)}, f32[4,1024,1024]{2,1,0:T(8,128)}, u32[]{:S(2)}, u32[]{:S(2)}) %collective-permute-start.1) | collective-permute-done | bytes 16777248 | tf_op jit(solution)/shard_map/while/body/eval_jaxpr/ppermute | solution.py:14
  2775.7 12.8 multiply_reduce_fusion
  2788.5 14.3 fusion.39
  2802.9 18.8 fusion.36
  2902.4 7.9 fusion.63
  2936.7 8.3 fusion.66
  2958.3 20.6 multiply_reduce_fusion.1
  2978.9 11.3 convolution_convert_fusion.1
  3004.2 10.0 broadcast_multiply_fusion.1
  3052.4 17.5 convolution_convert_fusion
  3071.5 8.2 fusion.81
  3079.7 9.0 fusion.84
  3088.7 9.7 fusion.87
  3106.8 11.2 fusion.2
  3119.0 194.8 %reduce-scatter.3.cloned.1.call-done = bf16[256,8192]{1,0:T(8,128)(2,1)} async-done(((bf16[2048,8192]{1,0:T(8,128)(2,1)}), bf16[256,8192]{1,0:T(8,128)(2,1)}) %reduce-scatter.3.cloned.1.call-update) | async-done | bytes 4194320 | tf_op jit(solution)/shard_map/reduce_scatter | solution.py:244
  3314.0 12.7 fusion.53
  3326.7 15.3 fusion.71
  3342.9 41.4 %all-reduce.15 = (f32[2048]{0:T(1024)}, f32[4096]{0:T(1024)}, f32[8]{0:T(128)}, f32[4096]{0:T(1024)}, f32[4096]{0:T(1024)}) all-reduce(f32[2048]{0:T(1024)S(1)} %get-tuple-element.147, f32[4096]{0:T(1024)S(1)} %get-tuple-element.193, f32[8]{0:T(128)S(1)} %fusion.106, ...), channel_id=1, replica_groups=mesh['dp'=8,'ctx'=4] {'dp','ctx'}, use_global_device_ids=true, to_apply=%region_25.26 | all-reduce | flops 14344 | bytes 114752 | tf_op jit(solution)/shard_map/psum | solution.py:265
  3387.7 95.7 %all-reduce.21.cloned.1.call-done = (f32[4,4096]{1,0:T(4,128)}, f32[3,4,4,4,256]{2,3,4,1,0:T(4,128)}, f32[8,12288]{1,0:T(8,128)}) async-done(((f32[4,4096]{1,0:T(4,128)}, f32[3,4,4,4,256]{2,3,4,1,0:T(4,128)}, f32[8,12288]{1,0:T(8,128)}), (f32[4,4096]{1,0:T(4,128)}, f32[3,4,4,4,256]{2,3,4,1,0:T(4,128)}, f32[8,12288]{1,0:T(8,128)})) %all-reduce.21.cloned.1.call-update) | async-done | bytes 655376 | tf_op jit(solution)/shard_map/psum | solution.py:265
  3489.5 219.5 %all-reduce.23.cloned.1.call-done = (bf16[256,8192]{1,0:T(8,128)(2,1)}, bf16[512,2048]{1,0:T(8,128)(2,1)}) async-done(((bf16[256,8192]{1,0:T(8,128)(2,1)}, bf16[512,2048]{1,0:T(8,128)(2,1)}), (bf16[256,8192]{1,0:T(8,128)(2,1)}, bf16[512,2048]{1,0:T(8,128)(2,1)})) %all-reduce.23.cloned.1.call-update) | async-done | bytes 6291472 | tf_op jit(solution)/shard_map/psum | solution.py:262
  (335 shorter events, 326.2 us)
Async XLA Ops:
  7.2 321.9 %copy-start = (bf16[8,12288]{1,0:T(8,128)(2,1)S(1)}, bf16[8,12288]{1,0:T(8,128)(2,1)}, u32[]{:S(2)}) copy-start(bf16[8,12288]{1,0:T(8,128)(2,1)} %param.24) | copy-start | bytes 589828
  7.3 166.2 %all-gather.3.cloned.1.call-start = ((), (), s32[]{:S(2)}) async-start(), calls=%async_computation.2 | async-start | bytes 37748736 | tf_op jit(solution)/shard_map/all_gather | solution.py:153
  8.0 257.3 %all-gather.5.cloned.1.call-start = ((), (), s32[]{:S(2)}) async-start(), calls=%async_computation.3 | async-start | bytes 18874368 | tf_op jit(solution)/shard_map/all_gather | solution.py:187
  8.8 3110.2 %reduce-scatter.5.cloned.1.call-start = ((), (), s32[]{:S(2)}) async-start(), calls=%async_computation.5 | async-start | bytes 18874368 | tf_op jit(solution)/shard_map/reduce_scatter | solution.py:253
  10.0 183.3 %copy-start.50 = (f32[2048]{0:T(1024)}, f32[2048]{0:T(1024)S(1)}, u32[]{:S(2)}) copy-start(f32[2048]{0:T(1024)S(1)} %convert_element_type.143) | copy-start | bytes 24580
  10.0 255.3 %copy-start.71 = (f32[4096]{0:T(1024)}, f32[4096]{0:T(1024)S(1)}, u32[]{:S(2)}) copy-start(f32[4096]{0:T(1024)S(1)} %convert_element_type.162) | copy-start | bytes 49156
  14.3 195.9 %copy-start.36 = (bf16[1,4,4,4,256]{2,3,4,1,0:T(4,128)(2,1)}, bf16[1,4,4,4,256]{2,3,4,1,0:T(4,128)(2,1)S(1)}, u32[]{:S(2)}) copy-start(bf16[1,4,4,4,256]{2,3,4,1,0:T(4,128)(2,1)S(1)} %copy.127) | copy-start | bytes 98308
  14.5 178.7 %copy-start.57 = (f32[256]{0:T(256)}, f32[256]{0:T(256)S(1)}, u32[]{:S(2)}) copy-start(f32[256]{0:T(256)S(1)} %broadcast_multiply_fusion.6) | copy-start | bytes 3076
  15.0 178.3 %copy-start.59 = (f32[256]{0:T(256)}, f32[256]{0:T(256)S(1)}, u32[]{:S(2)}) copy-start(f32[256]{0:T(256)S(1)} %fusion.114) | copy-start | bytes 3076
  15.4 177.9 %copy-start.46 = (bf16[256,2048]{1,0:T(8,128)(2,1)}, bf16[256,2048]{1,0:T(8,128)(2,1)S(1)}, u32[]{:S(2)}) copy-start(bf16[256,2048]{1,0:T(8,128)(2,1)S(1)} %fusion.57) | copy-start | bytes 3145732
  16.4 265.1 %copy-start.61 = (f32[1,4096]{1,0:T(1,128)}, f32[1,4096]{1,0:T(1,128)S(1)}, u32[]{:S(2)}) copy-start(f32[1,4096]{1,0:T(1,128)S(1)} %get-tuple-element.212) | copy-start | bytes 49156
  16.4 265.1 %copy-start.63 = (f32[1,4096]{1,0:T(1,128)}, f32[1,4096]{1,0:T(1,128)S(1)}, u32[]{:S(2)}) copy-start(f32[1,4096]{1,0:T(1,128)S(1)} %get-tuple-element.213) | copy-start | bytes 49156
  16.4 265.1 %copy-start.65 = (f32[1,4096]{1,0:T(1,128)}, f32[1,4096]{1,0:T(1,128)S(1)}, u32[]{:S(2)}) copy-start(f32[1,4096]{1,0:T(1,128)S(1)} %get-tuple-element.214) | copy-start | bytes 49156
  16.5 265.1 %copy-start.67 = (f32[1,4096]{1,0:T(1,128)}, f32[1,4096]{1,0:T(1,128)S(1)}, u32[]{:S(2)}) copy-start(f32[1,4096]{1,0:T(1,128)S(1)} %get-tuple-element.215) | copy-start | bytes 49156
  194.8 86.7 %collective-permute-start.2 = (bf16[3,4096]{1,0:T(4,128)(2,1)}, bf16[3,4096]{1,0:T(4,128)(2,1)S(1)}, u32[]{:S(2)}, u32[]{:S(2)}) collective-permute-start(bf16[3,4096]{1,0:T(4,128)(2,1)} %slice.91), channel_id=1, source_target_pairs={{0,1},{1,2},{2,3},{4,5},{5,6},{6,7},{8,9},{9,10},{10,11},{12,13},{... | collective-permute-start | bytes 73736 | tf_op jit(solution)/shard_map/ppermute | solution.py:14
  211.4 53.9 %copy-start.47 = (bf16[1,256,2048]{2,1,0:T(8,128)(2,1)S(1)}, bf16[1,256,2048]{2,1,0:T(8,128)(2,1)}, u32[]{:S(2)}) copy-start(bf16[1,256,2048]{2,1,0:T(8,128)(2,1)} %param.29) | copy-start | bytes 3145732
  211.4 53.9 %copy-start.86 = (f32[256]{0:T(256)S(1)}, f32[256]{0:T(256)}, u32[]{:S(2)}) copy-start(f32[256]{0:T(256)} %compare_convert_fusion) | copy-start | bytes 3076
  354.7 1214.6 %copy-start.45 = (bf16[4,256,256]{2,1,0:T(8,128)(2,1)}, bf16[4,256,256]{2,1,0:T(8,128)(2,1)S(1)}, u32[]{:S(2)}) copy-start(bf16[4,256,256]{2,1,0:T(8,128)(2,1)S(1)} %get-tuple-element.229) | copy-start | bytes 1572868
  355.0 32.1 copy-start.26
  412.4 363.6 %collective-permute-start = (f32[4,1024,1024]{2,1,0:T(8,128)}, f32[4,1024,1024]{2,1,0:T(8,128)}, u32[]{:S(2)}, u32[]{:S(2)}) collective-permute-start(f32[4,1024,1024]{2,1,0:T(8,128)} %multiply_add_fusion.10), channel_id=1, source_target_pairs={{0,1},{1,2},{2,3},{4,5},{5,6},{6,7},{8,9},{9,10},{10,11},{12,13},{... | collective-permute-start | bytes 50331656 | tf_op jit(solution)/shard_map/while/body/eval_jaxpr/ppermute | solution.py:14
  793.3 363.8 %collective-permute-start = (f32[4,1024,1024]{2,1,0:T(8,128)}, f32[4,1024,1024]{2,1,0:T(8,128)}, u32[]{:S(2)}, u32[]{:S(2)}) collective-permute-start(f32[4,1024,1024]{2,1,0:T(8,128)} %multiply_add_fusion.10), channel_id=1, source_target_pairs={{0,1},{1,2},{2,3},{4,5},{5,6},{6,7},{8,9},{9,10},{10,11},{12,13},{... | collective-permute-start | bytes 50331656 | tf_op jit(solution)/shard_map/while/body/eval_jaxpr/ppermute | solution.py:14
  1174.4 362.8 %collective-permute-start = (f32[4,1024,1024]{2,1,0:T(8,128)}, f32[4,1024,1024]{2,1,0:T(8,128)}, u32[]{:S(2)}, u32[]{:S(2)}) collective-permute-start(f32[4,1024,1024]{2,1,0:T(8,128)} %multiply_add_fusion.10), channel_id=1, source_target_pairs={{0,1},{1,2},{2,3},{4,5},{5,6},{6,7},{8,9},{9,10},{10,11},{12,13},{... | collective-permute-start | bytes 50331656 | tf_op jit(solution)/shard_map/while/body/eval_jaxpr/ppermute | solution.py:14
  1569.3 12.2 copy-start.17
  1587.7 25.6 copy-start.14
  1656.7 362.7 %collective-permute-start.1 = (f32[4,1024,1024]{2,1,0:T(8,128)}, f32[4,1024,1024]{2,1,0:T(8,128)}, u32[]{:S(2)}, u32[]{:S(2)}) collective-permute-start(f32[4,1024,1024]{2,1,0:T(8,128)} %multiply_add_fusion.11), channel_id=1, source_target_pairs={{1,0},{2,1},{3,2},{5,4},{6,5},{7,6},{9,8},{10,9},{11,10},{13,12},{... | collective-permute-start | bytes 50331656 | tf_op jit(solution)/shard_map/while/body/eval_jaxpr/ppermute | solution.py:14
  2036.7 361.3 %collective-permute-start.1 = (f32[4,1024,1024]{2,1,0:T(8,128)}, f32[4,1024,1024]{2,1,0:T(8,128)}, u32[]{:S(2)}, u32[]{:S(2)}) collective-permute-start(f32[4,1024,1024]{2,1,0:T(8,128)} %multiply_add_fusion.11), channel_id=1, source_target_pairs={{1,0},{2,1},{3,2},{5,4},{6,5},{7,6},{9,8},{10,9},{11,10},{13,12},{... | collective-permute-start | bytes 50331656 | tf_op jit(solution)/shard_map/while/body/eval_jaxpr/ppermute | solution.py:14
  2415.3 360.4 %collective-permute-start.1 = (f32[4,1024,1024]{2,1,0:T(8,128)}, f32[4,1024,1024]{2,1,0:T(8,128)}, u32[]{:S(2)}, u32[]{:S(2)}) collective-permute-start(f32[4,1024,1024]{2,1,0:T(8,128)} %multiply_add_fusion.11), channel_id=1, source_target_pairs={{1,0},{2,1},{3,2},{5,4},{6,5},{7,6},{9,8},{10,9},{11,10},{13,12},{... | collective-permute-start | bytes 50331656 | tf_op jit(solution)/shard_map/while/body/eval_jaxpr/ppermute | solution.py:14
  2775.7 12.8 copy-start.2
  2775.7 12.8 copy-start.27
  2775.7 12.9 copy-start.55
  2788.5 14.3 copy-start.12
  2865.3 11.6 copy-start.83
  2958.3 20.7 copy-start.48
  2958.3 20.6 copy-start.87
  2978.9 11.3 copy-start.34
  2990.2 323.6 %reduce-scatter.3.cloned.1.call-start = ((), (), s32[]{:S(2)}) async-start(), calls=%async_computation.4 | async-start | bytes 37748736 | tf_op jit(solution)/shard_map/reduce_scatter | solution.py:244
  3014.1 11.2 copy-start.22
  3023.8 22.4 collective-permute-start.3
  3069.9 413.6 %all-reduce.21.cloned.1.call-start = ((), (), s32[]{:S(2)}) async-start(), calls=%async_computation.6 | async-start | bytes 13500416 | tf_op jit(solution)/shard_map/psum | solution.py:265
  3088.7 17.5 copy-start.79
  3088.7 17.5 copy-start.81
  3106.8 11.2 copy-start.74
  3118.7 195.2 %copy-start.35 = (bf16[256,4096]{1,0:T(8,128)(2,1)S(1)}, bf16[256,4096]{1,0:T(8,128)(2,1)}, u32[]{:S(2)}) copy-start(bf16[256,4096]{1,0:T(8,128)(2,1)} %copy-done.34) | copy-start | bytes 6291460
  3118.7 195.2 %copy-start.88 = (f32[256]{0:T(256)S(1)}, f32[256]{0:T(256)}, u32[]{:S(2)}) copy-start(f32[256]{0:T(256)} %compare_convert_fusion) | copy-start | bytes 3076
  3118.7 590.2 %all-reduce.23.cloned.1.call-start = ((), (), s32[]{:S(2)}) async-start(), calls=%async_computation.7 | async-start | bytes 12582912 | tf_op jit(solution)/shard_map/psum | solution.py:262
  3314.0 12.7 copy-start.43
  3314.0 12.7 copy-start.44
  3326.7 15.3 copy-start.90
  (63 other events, 352.4 us)
Sparse Core Ops, SparseCore 0:
  10.0 163.4 all-gather.2
  175.4 89.8 all-gather.4
  2990.3 114.7 reduce-scatter.4
  3108.5 205.2 reduce-scatter.2
  3321.5 161.8 all-reduce.20
  3485.8 223.0 all-reduce.22
where the time goes:
time: 3730 us
  waiting for transfers between devices  2860 us (77%)
  matrix products  346 us (9%)
  other arithmetic  244 us (7%)
  local copies, waits for them, and re-layouts  180 us (5%)
  blocking collectives  41.4 us (1%)
  starting transfers between devices  38.6 us (1%)
    ppermute x8, waiting for transfers between devices, shifted(): return lax.ppermute(x, axis, pairs)  2140 us
    psum x1, waiting for transfers between devices, on_device(): lax.psum(up_part, 'ctx').astype(jnp.float32)  219 us
    reduce_scatter x1, waiting for transfers between devices, on_device(): lax.psum_scatter(lax.dot_general(columns, upward_grad, contract_first, pr...  195 us
    all_gather x1, waiting for transfers between devices, on_device(): lax.all_gather(up_weight, 'dp', axis=0, tiled=True)  157 us
    psum x1, waiting for transfers between devices, on_device(): lax.psum((norm_scale_grad, conv_taps_grad, conv_shift_grad, qkv_grad, gat...  95.7 us
  transfers between devices with their start and end apart: 14, of which 11 were waited for; matrix products, arithmetic and copies ran while one was open for 6% of the time, Pallas kernels for 0%

commit v1 on v0

--- a/solution.py
+++ b/solution.py
@@ -259,7 +259,7 @@
         tiled=True,
     )
     up_total, down_total = (
-        lax.psum(up_part, "ctx").astype(jnp.float32),
+        jnp.sum(lax.all_gather(up_part, "ctx"), axis=0).astype(jnp.float32),
         lax.psum(down_part, "ctx").astype(jnp.float32),
     )
     small_total = lax.psum(

time: 3730 us -> 3890 us (1.043)
  waiting for transfers between devices: 2860 us -> 3010 us
    all_gather x0 -> x1, waiting for transfers between devices: none -> 283 us  [on_device(): lax.all_gather(up_part, 'ctx')]
    psum x1, waiting for transfers between devices: 219 us -> 82.7 us  [on_device(): lax.psum(down_part, 'ctx').astype(jnp.float32)]
  transfers between devices with their start and end apart: 14 -> 15, of which waited for: 11 -> 12; matrix products, arithmetic and copies ran while one was open for 6% -> 6% of each run, Pallas kernels for 0% -> 0%
where the time goes in v1:
time: 3890 us
  waiting for transfers between devices  3010 us (77%)
  matrix products  346 us (9%)
  other arithmetic  256 us (7%)
  local copies, waits for them, and re-layouts  180 us (5%)
  blocking collectives  41.3 us (1%)
    ppermute x8, waiting for transfers between devices, shifted(): return lax.ppermute(x, axis, pairs)  2140 us
    all_gather x1, waiting for transfers between devices, on_device(): lax.all_gather(up_part, 'ctx')  283 us
    reduce_scatter x1, waiting for transfers between devices, on_device(): lax.psum_scatter(lax.dot_general(columns, upward_grad, contract_first, pr...  194 us
    all_gather x1, waiting for transfers between devices, on_device(): lax.all_gather(up_weight, 'dp', axis=0, tiled=True)  157 us
    psum x1, waiting for transfers between devices, on_device(): lax.psum((norm_scale_grad, conv_taps_grad, conv_shift_grad, qkv_grad, gat...  95.8 us
    psum x1, waiting for transfers between devices, on_device(): lax.psum(down_part, 'ctx').astype(jnp.float32)  82.7 us
  transfers between devices with their start and end apart: 15, of which 12 were waited for; matrix products, arithmetic and copies ran while one was open for 6% of the time, Pallas kernels for 0%

profile of v1, /device:TPU:0, one launch (start us, length us, event | category | flops | bytes accessed | tf_op | source)
XLA Modules:
  0.0 3885.6 jit_solution(16148270998035721203)
XLA Ops:
  16.4 157.1 %all-gather.5.cloned.1.call-done = bf16[2048,8192]{1,0:T(8,128)(2,1)} async-done(((bf16[256,8192]{1,0:T(8,128)(2,1)}), bf16[2048,8192]{1,0:T(8,128)(2,1)}) %all-gather.5.cloned.1.call-update) | async-done | bytes 33554448 | tf_op jit(solution)/shard_map/all_gather | solution.py:153
  173.5 19.8 fusion.142
  214.3 51.0 %all-gather.7.cloned.1.call-done = bf16[4096,2048]{1,0:T(8,128)(2,1)} async-done(((bf16[512,2048]{1,0:T(8,128)(2,1)}), bf16[4096,2048]{1,0:T(8,128)(2,1)}) %all-gather.7.cloned.1.call-update) | async-done | bytes 16777232 | tf_op jit(solution)/shard_map/all_gather | solution.py:187
  265.3 12.2 broadcast_multiply_fusion
  344.1 10.2 fusion.100
  357.5 29.5 fusion.54
  394.9 1142.1 %while.24 = (s32[]{:T(128)}, f32[4,1024,1024]{2,1,0:T(8,128)}, f32[4,1,1]{0,2,1:T(1,128)S(1)}, f32[4,1024,1024]{2,1,0:T(8,128)}, s32[]{:T(128)}) while((s32[]{:T(128)}, f32[4,1024,1024]{2,1,0:T(8,128)}, f32[4,1,1]{0,2,1:T(1,128)S(1)}, f32[4,1024,1024]{2,1,0:T(8,128)}, s32[]{:T(128)}) %tuple.134), condition=%wide.region_5.6_spmd, body=%wide.region_4.5_spmd.sunk | while | flops 8388610 | bytes 117440624 | solution.py:170
  394.9 17.3 multiply_add_fusion.10
  412.2 9.2 collective-permute-start
  421.4 354.4 %collective-permute-done = f32[4,1024,1024]{2,1,0:T(8,128)} collective-permute-done((f32[4,1024,1024]{2,1,0:T(8,128)}, f32[4,1024,1024]{2,1,0:T(8,128)}, u32[]{:S(2)}, u32[]{:S(2)}) %collective-permute-start) | collective-permute-done | bytes 16777248 | tf_op jit(solution)/shard_map/while/body/eval_jaxpr/ppermute | solution.py:14
  775.8 17.3 multiply_add_fusion.10
  793.1 10.2 collective-permute-start
  803.3 353.6 %collective-permute-done = f32[4,1024,1024]{2,1,0:T(8,128)} collective-permute-done((f32[4,1024,1024]{2,1,0:T(8,128)}, f32[4,1024,1024]{2,1,0:T(8,128)}, u32[]{:S(2)}, u32[]{:S(2)}) %collective-permute-start) | collective-permute-done | bytes 16777248 | tf_op jit(solution)/shard_map/while/body/eval_jaxpr/ppermute | solution.py:14
  1156.9 17.3 multiply_add_fusion.10
  1174.2 10.2 collective-permute-start
  1184.4 352.7 %collective-permute-done = f32[4,1024,1024]{2,1,0:T(8,128)} collective-permute-done((f32[4,1024,1024]{2,1,0:T(8,128)}, f32[4,1024,1024]{2,1,0:T(8,128)}, u32[]{:S(2)}, u32[]{:S(2)}) %collective-permute-start) | collective-permute-done | bytes 16777248 | tf_op jit(solution)/shard_map/while/body/eval_jaxpr/ppermute | solution.py:14
  1537.0 9.3 convert_element_type.162
  1547.1 21.8 fusion.1
  1568.9 12.2 fusion.143
  1591.4 21.5 fusion
  1612.9 18.4 fusion.4
  1639.2 1136.2 %while.25 = (s32[]{:T(128)}, f32[4,1024,1024]{2,1,0:T(8,128)}, f32[4,1,1]{0,2,1:T(1,128)S(1)}, f32[4,1024,1024]{2,1,0:T(8,128)}, s32[]{:T(128)}) while((s32[]{:T(128)}, f32[4,1024,1024]{2,1,0:T(8,128)}, f32[4,1,1]{0,2,1:T(1,128)S(1)}, f32[4,1024,1024]{2,1,0:T(8,128)}, s32[]{:T(128)}) %tuple.135), condition=%wide.region_11.12_spmd, body=%wide.region_10.11_spmd.sunk | while | flops 8388610 | bytes 117440624 | solution.py:209
  1639.2 17.3 multiply_add_fusion.11
  1657.8 361.4 %collective-permute-done.1 = f32[4,1024,1024]{2,1,0:T(8,128)} collective-permute-done((f32[4,1024,1024]{2,1,0:T(8,128)}, f32[4,1024,1024]{2,1,0:T(8,128)}, u32[]{:S(2)}, u32[]{:S(2)}) %collective-permute-start.1) | collective-permute-done | bytes 16777248 | tf_op jit(solution)/shard_map/while/body/eval_jaxpr/ppermute | solution.py:14
  2019.2 17.3 multiply_add_fusion.11
  2037.7 360.0 %collective-permute-done.1 = f32[4,1024,1024]{2,1,0:T(8,128)} collective-permute-done((f32[4,1024,1024]{2,1,0:T(8,128)}, f32[4,1024,1024]{2,1,0:T(8,128)}, u32[]{:S(2)}, u32[]{:S(2)}) %collective-permute-start.1) | collective-permute-done | bytes 16777248 | tf_op jit(solution)/shard_map/while/body/eval_jaxpr/ppermute | solution.py:14
  2397.7 17.3 multiply_add_fusion.11
  2416.3 359.1 %collective-permute-done.1 = f32[4,1024,1024]{2,1,0:T(8,128)} collective-permute-done((f32[4,1024,1024]{2,1,0:T(8,128)}, f32[4,1024,1024]{2,1,0:T(8,128)}, u32[]{:S(2)}, u32[]{:S(2)}) %collective-permute-start.1) | collective-permute-done | bytes 16777248 | tf_op jit(solution)/shard_map/while/body/eval_jaxpr/ppermute | solution.py:14
  2775.4 12.8 multiply_reduce_fusion
  2788.3 14.0 fusion.39
  2802.3 18.9 fusion.36
  2936.3 8.1 fusion.66
  2957.6 20.5 multiply_reduce_fusion.1
  2978.1 11.3 convolution_convert_fusion.1
  3003.4 9.9 broadcast_multiply_fusion.1
  3051.6 17.4 convolution_convert_fusion
  3070.6 8.2 fusion.81
  3078.8 9.2 fusion.84
  3088.0 9.7 fusion.87
  3106.1 11.2 fusion.2
  3118.9 194.1 %reduce-scatter.3.cloned.1.call-done = bf16[256,8192]{1,0:T(8,128)(2,1)} async-done(((bf16[2048,8192]{1,0:T(8,128)(2,1)}), bf16[256,8192]{1,0:T(8,128)(2,1)}) %reduce-scatter.3.cloned.1.call-update) | async-done | bytes 4194320 | tf_op jit(solution)/shard_map/reduce_scatter | solution.py:244
  3313.2 12.7 fusion.53
  3325.9 15.3 fusion.71
  3342.1 41.3 %all-reduce.15 = (f32[2048]{0:T(1024)}, f32[4096]{0:T(1024)}, f32[8]{0:T(128)}, f32[4096]{0:T(1024)}, f32[4096]{0:T(1024)}) all-reduce(f32[2048]{0:T(1024)S(1)} %get-tuple-element.147, f32[4096]{0:T(1024)S(1)} %get-tuple-element.191, f32[8]{0:T(128)S(1)} %fusion.106, ...), channel_id=1, replica_groups=mesh['dp'=8,'ctx'=4] {'dp','ctx'}, use_global_device_ids=true, to_apply=%region_25.26 | all-reduce | flops 14344 | bytes 114752 | tf_op jit(solution)/shard_map/psum | solution.py:265
  3386.8 95.8 %all-reduce.22.cloned.1.call-done = (f32[4,4096]{1,0:T(4,128)}, f32[3,4,4,4,256]{2,3,4,1,0:T(4,128)}, f32[8,12288]{1,0:T(8,128)}) async-done(((f32[4,4096]{1,0:T(4,128)}, f32[3,4,4,4,256]{2,3,4,1,0:T(4,128)}, f32[8,12288]{1,0:T(8,128)}), (f32[4,4096]{1,0:T(4,128)}, f32[3,4,4,4,256]{2,3,4,1,0:T(4,128)}, f32[8,12288]{1,0:T(8,128)})) %all-reduce.22.cloned.1.call-update) | async-done | bytes 655376 | tf_op jit(solution)/shard_map/psum | solution.py:265
  3488.7 82.7 %all-reduce.20.cloned.1.call-done = bf16[512,2048]{1,0:T(8,128)(2,1)} async-done(((bf16[512,2048]{1,0:T(8,128)(2,1)}), bf16[512,2048]{1,0:T(8,128)(2,1)}) %all-reduce.20.cloned.1.call-update) | async-done | bytes 2097168 | tf_op jit(solution)/shard_map/psum | solution.py:263
  3575.5 283.2 %all-gather.9.cloned.1.call-done = bf16[1024,8192]{1,0:T(8,128)(2,1)} async-done(((bf16[256,8192]{1,0:T(8,128)(2,1)}), bf16[1024,8192]{1,0:T(8,128)(2,1)}) %all-gather.9.cloned.1.call-update) | async-done | bytes 16777232 | tf_op jit(solution)/shard_map/all_gather | solution.py:262
  3858.7 11.8 reduce_sum.258
  (337 shorter events, 344.1 us)
Async XLA Ops:
  7.2 321.5 %copy-start = (bf16[8,12288]{1,0:T(8,128)(2,1)S(1)}, bf16[8,12288]{1,0:T(8,128)(2,1)}, u32[]{:S(2)}) copy-start(bf16[8,12288]{1,0:T(8,128)(2,1)} %param.24) | copy-start | bytes 589828
  7.3 166.2 %all-gather.5.cloned.1.call-start = ((), (), s32[]{:S(2)}) async-start(), calls=%async_computation.2 | async-start | bytes 37748736 | tf_op jit(solution)/shard_map/all_gather | solution.py:153
  8.0 257.3 %all-gather.7.cloned.1.call-start = ((), (), s32[]{:S(2)}) async-start(), calls=%async_computation.3 | async-start | bytes 18874368 | tf_op jit(solution)/shard_map/all_gather | solution.py:187
  8.8 3109.4 %reduce-scatter.5.cloned.1.call-start = ((), (), s32[]{:S(2)}) async-start(), calls=%async_computation.5 | async-start | bytes 18874368 | tf_op jit(solution)/shard_map/reduce_scatter | solution.py:253
  10.0 183.3 %copy-start.49 = (f32[2048]{0:T(1024)}, f32[2048]{0:T(1024)S(1)}, u32[]{:S(2)}) copy-start(f32[2048]{0:T(1024)S(1)} %convert_element_type.145) | copy-start | bytes 24580
  10.0 255.3 %copy-start.70 = (f32[4096]{0:T(1024)}, f32[4096]{0:T(1024)S(1)}, u32[]{:S(2)}) copy-start(f32[4096]{0:T(1024)S(1)} %convert_element_type.164) | copy-start | bytes 49156
  14.3 196.1 %copy-start.36 = (bf16[1,4,4,4,256]{2,3,4,1,0:T(4,128)(2,1)}, bf16[1,4,4,4,256]{2,3,4,1,0:T(4,128)(2,1)S(1)}, u32[]{:S(2)}) copy-start(bf16[1,4,4,4,256]{2,3,4,1,0:T(4,128)(2,1)S(1)} %copy.127) | copy-start | bytes 98308
  14.5 178.8 %copy-start.56 = (f32[256]{0:T(256)}, f32[256]{0:T(256)S(1)}, u32[]{:S(2)}) copy-start(f32[256]{0:T(256)S(1)} %broadcast_multiply_fusion.6) | copy-start | bytes 3076
  15.0 178.3 %copy-start.58 = (f32[256]{0:T(256)}, f32[256]{0:T(256)S(1)}, u32[]{:S(2)}) copy-start(f32[256]{0:T(256)S(1)} %fusion.114) | copy-start | bytes 3076
  15.4 177.9 %copy-start.46 = (bf16[256,2048]{1,0:T(8,128)(2,1)}, bf16[256,2048]{1,0:T(8,128)(2,1)S(1)}, u32[]{:S(2)}) copy-start(bf16[256,2048]{1,0:T(8,128)(2,1)S(1)} %fusion.57) | copy-start | bytes 3145732
  16.3 265.1 %copy-start.60 = (f32[1,4096]{1,0:T(1,128)}, f32[1,4096]{1,0:T(1,128)S(1)}, u32[]{:S(2)}) copy-start(f32[1,4096]{1,0:T(1,128)S(1)} %get-tuple-element.210) | copy-start | bytes 49156
  16.3 265.1 %copy-start.62 = (f32[1,4096]{1,0:T(1,128)}, f32[1,4096]{1,0:T(1,128)S(1)}, u32[]{:S(2)}) copy-start(f32[1,4096]{1,0:T(1,128)S(1)} %get-tuple-element.211) | copy-start | bytes 49156
  16.3 265.1 %copy-start.64 = (f32[1,4096]{1,0:T(1,128)}, f32[1,4096]{1,0:T(1,128)S(1)}, u32[]{:S(2)}) copy-start(f32[1,4096]{1,0:T(1,128)S(1)} %get-tuple-element.212) | copy-start | bytes 49156
  16.4 265.1 %copy-start.66 = (f32[1,4096]{1,0:T(1,128)}, f32[1,4096]{1,0:T(1,128)S(1)}, u32[]{:S(2)}) copy-start(f32[1,4096]{1,0:T(1,128)S(1)} %get-tuple-element.213) | copy-start | bytes 49156
  194.8 86.6 %collective-permute-start.2 = (bf16[3,4096]{1,0:T(4,128)(2,1)}, bf16[3,4096]{1,0:T(4,128)(2,1)S(1)}, u32[]{:S(2)}, u32[]{:S(2)}) collective-permute-start(bf16[3,4096]{1,0:T(4,128)(2,1)} %slice.91), channel_id=1, source_target_pairs={{0,1},{1,2},{2,3},{4,5},{5,6},{6,7},{8,9},{9,10},{10,11},{12,13},{... | collective-permute-start | bytes 73736 | tf_op jit(solution)/shard_map/ppermute | solution.py:14
  211.6 53.7 %copy-start.47 = (bf16[1,256,2048]{2,1,0:T(8,128)(2,1)S(1)}, bf16[1,256,2048]{2,1,0:T(8,128)(2,1)}, u32[]{:S(2)}) copy-start(bf16[1,256,2048]{2,1,0:T(8,128)(2,1)} %param.29) | copy-start | bytes 3145732
  211.6 53.7 %copy-start.85 = (f32[256]{0:T(256)S(1)}, f32[256]{0:T(256)}, u32[]{:S(2)}) copy-start(f32[256]{0:T(256)} %compare_convert_fusion) | copy-start | bytes 3076
  354.4 1214.5 %copy-start.45 = (bf16[4,256,256]{2,1,0:T(8,128)(2,1)}, bf16[4,256,256]{2,1,0:T(8,128)(2,1)S(1)}, u32[]{:S(2)}) copy-start(bf16[4,256,256]{2,1,0:T(8,128)(2,1)S(1)} %get-tuple-element.227) | copy-start | bytes 1572868
  354.7 32.3 copy-start.26
  412.2 363.6 %collective-permute-start = (f32[4,1024,1024]{2,1,0:T(8,128)}, f32[4,1024,1024]{2,1,0:T(8,128)}, u32[]{:S(2)}, u32[]{:S(2)}) collective-permute-start(f32[4,1024,1024]{2,1,0:T(8,128)} %multiply_add_fusion.10), channel_id=1, source_target_pairs={{0,1},{1,2},{2,3},{4,5},{5,6},{6,7},{8,9},{9,10},{10,11},{12,13},{... | collective-permute-start | bytes 50331656 | tf_op jit(solution)/shard_map/while/body/eval_jaxpr/ppermute | solution.py:14
  793.1 363.8 %collective-permute-start = (f32[4,1024,1024]{2,1,0:T(8,128)}, f32[4,1024,1024]{2,1,0:T(8,128)}, u32[]{:S(2)}, u32[]{:S(2)}) collective-permute-start(f32[4,1024,1024]{2,1,0:T(8,128)} %multiply_add_fusion.10), channel_id=1, source_target_pairs={{0,1},{1,2},{2,3},{4,5},{5,6},{6,7},{8,9},{9,10},{10,11},{12,13},{... | collective-permute-start | bytes 50331656 | tf_op jit(solution)/shard_map/while/body/eval_jaxpr/ppermute | solution.py:14
  1174.2 362.8 %collective-permute-start = (f32[4,1024,1024]{2,1,0:T(8,128)}, f32[4,1024,1024]{2,1,0:T(8,128)}, u32[]{:S(2)}, u32[]{:S(2)}) collective-permute-start(f32[4,1024,1024]{2,1,0:T(8,128)} %multiply_add_fusion.10), channel_id=1, source_target_pairs={{0,1},{1,2},{2,3},{4,5},{5,6},{6,7},{8,9},{9,10},{10,11},{12,13},{... | collective-permute-start | bytes 50331656 | tf_op jit(solution)/shard_map/while/body/eval_jaxpr/ppermute | solution.py:14
  1568.9 12.2 copy-start.17
  1587.3 25.6 copy-start.14
  1656.5 362.7 %collective-permute-start.1 = (f32[4,1024,1024]{2,1,0:T(8,128)}, f32[4,1024,1024]{2,1,0:T(8,128)}, u32[]{:S(2)}, u32[]{:S(2)}) collective-permute-start(f32[4,1024,1024]{2,1,0:T(8,128)} %multiply_add_fusion.11), channel_id=1, source_target_pairs={{1,0},{2,1},{3,2},{5,4},{6,5},{7,6},{9,8},{10,9},{11,10},{13,12},{... | collective-permute-start | bytes 50331656 | tf_op jit(solution)/shard_map/while/body/eval_jaxpr/ppermute | solution.py:14
  2036.5 361.3 %collective-permute-start.1 = (f32[4,1024,1024]{2,1,0:T(8,128)}, f32[4,1024,1024]{2,1,0:T(8,128)}, u32[]{:S(2)}, u32[]{:S(2)}) collective-permute-start(f32[4,1024,1024]{2,1,0:T(8,128)} %multiply_add_fusion.11), channel_id=1, source_target_pairs={{1,0},{2,1},{3,2},{5,4},{6,5},{7,6},{9,8},{10,9},{11,10},{13,12},{... | collective-permute-start | bytes 50331656 | tf_op jit(solution)/shard_map/while/body/eval_jaxpr/ppermute | solution.py:14
  2415.0 360.4 %collective-permute-start.1 = (f32[4,1024,1024]{2,1,0:T(8,128)}, f32[4,1024,1024]{2,1,0:T(8,128)}, u32[]{:S(2)}, u32[]{:S(2)}) collective-permute-start(f32[4,1024,1024]{2,1,0:T(8,128)} %multiply_add_fusion.11), channel_id=1, source_target_pairs={{1,0},{2,1},{3,2},{5,4},{6,5},{7,6},{9,8},{10,9},{11,10},{13,12},{... | collective-permute-start | bytes 50331656 | tf_op jit(solution)/shard_map/while/body/eval_jaxpr/ppermute | solution.py:14
  2775.4 12.8 copy-start.2
  2775.4 12.8 copy-start.27
  2775.4 12.9 copy-start.54
  2788.3 14.0 copy-start.12
  2864.7 11.8 copy-start.82
  2957.6 20.5 copy-start.48
  2957.6 20.5 copy-start.86
  2978.1 11.3 copy-start.34
  2989.4 323.6 %reduce-scatter.3.cloned.1.call-start = ((), (), s32[]{:S(2)}) async-start(), calls=%async_computation.4 | async-start | bytes 37748736 | tf_op jit(solution)/shard_map/reduce_scatter | solution.py:244
  3023.0 22.4 collective-permute-start.3
  3069.0 413.6 %all-reduce.22.cloned.1.call-start = ((), (), s32[]{:S(2)}) async-start(), calls=%async_computation.8 | async-start | bytes 13500416 | tf_op jit(solution)/shard_map/psum | solution.py:265
  3088.0 17.3 copy-start.78
  3088.0 17.3 copy-start.80
  3106.1 11.2 copy-start.73
  3118.1 195.1 %copy-start.35 = (bf16[256,4096]{1,0:T(8,128)(2,1)S(1)}, bf16[256,4096]{1,0:T(8,128)(2,1)}, u32[]{:S(2)}) copy-start(bf16[256,4096]{1,0:T(8,128)(2,1)} %copy-done.34) | copy-start | bytes 6291460
  3118.1 195.1 %copy-start.87 = (f32[256]{0:T(256)S(1)}, f32[256]{0:T(256)}, u32[]{:S(2)}) copy-start(f32[256]{0:T(256)} %compare_convert_fusion) | copy-start | bytes 3076
  3118.1 453.3 %all-reduce.20.cloned.1.call-start = ((), (), s32[]{:S(2)}) async-start(), calls=%async_computation.6 | async-start | bytes 4194304 | tf_op jit(solution)/shard_map/psum | solution.py:263
  3118.7 740.0 %all-gather.9.cloned.1.call-start = ((), (), s32[]{:S(2)}) async-start(), calls=%async_computation.7 | async-start | bytes 20971520 | tf_op jit(solution)/shard_map/all_gather | solution.py:262
  3313.1 12.7 copy-start.43
  3313.2 12.7 copy-start.44
  3325.8 15.3 copy-start.89
  (63 other events, 364.6 us)
Sparse Core Ops, SparseCore 0:
  10.0 163.4 all-gather.4
  175.4 89.8 all-gather.6
  2989.5 114.7 reduce-scatter.4
  3107.7 205.2 reduce-scatter.2
  3320.7 161.8 all-reduce.21
  3484.9 86.3 all-reduce.19
  3572.9 285.7 all-gather.8
